TPU v7x, 32 devices: a whole 2x2x4 slice. The times are simulated.
32 devices in a mesh: gx: 4 (over z), gy: 2 (over y), gz: 4 (over x, core).
Axes of the slice: x: 2, y: 2, z: 4, core: 2. Of those that a mesh axis runs over, the one named last changes fastest.
Arguments:
- pop_ratio: float32 [19, 8, 32, 512], P(None, 'gx', 'gy', 'gz'), may hold values from 0.7 to 1.3
- solid_flags: int32 [8, 32, 512], P('gx', 'gy', 'gz'), may hold values 0 or 1
- class_ids: int32 [8, 32, 512], P('gx', 'gy', 'gz'), may hold values from 0 to 7
- drag_table: float32 [8], replicated, may hold values from 0.05 to 1
- row_map: int32 [8, 32, 512], P('gx', 'gy', 'gz'), may hold values from 0 to 4095, as said below
- old_basis: float32 [32, 16384], P(None, ('gx', 'gy', 'gz')), may hold values from -6 to 6
- old_sigma: float32 [32], replicated, may hold values from 1 to 10
Outputs:
- final_populations: float32 [19, 8, 32, 512], P(None, 'gx', 'gy', 'gz')
- new_basis: float32 [44, 16384], P(None, ('gx', 'gy', 'gz'))
- triangle: float32 [44, 44], replicated
Inputs may be any that keep to these rules, and one draw needn't show every extreme that they name: `row_map`: within each slab along the first dimension every snapshot row is named by exactly 8 voxels, and the voxels of one device name rows of each block of 512 rows exactly 512 times.
All inputs are finite; a program needn't handle non-finite values. No bound on the sum of `solid_flags` on one device may be relied on, other than what follows from the above.
Results may differ from a plain program's by a relative error of at most 0.0003.
Values sent between devices are 32-bit elements; how exact they have to be, the bound alone decides.
No kernel may reach another device: no remote copies, remote signals or barrier semaphores. Data moves between devices by JAX's collectives and lax.ppermute only.
A program may use at most 64 MiB of HBM per device.

v0:
```python
import jax
import jax.numpy as jnp
import numpy as np
from jax import lax
from jax.sharding import PartitionSpec as P

STEPS = 4
VOX_ROW = 8
LATTICE = np.array(
    [
        [0, 0, 0],
        [1, 0, 0],
        [-1, 0, 0],
        [0, 1, 0],
        [0, -1, 0],
        [0, 0, 1],
        [0, 0, -1],
        [1, 1, 0],
        [-1, -1, 0],
        [1, -1, 0],
        [-1, 1, 0],
        [1, 0, 1],
        [-1, 0, -1],
        [1, 0, -1],
        [-1, 0, 1],
        [0, 1, 1],
        [0, -1, -1],
        [0, 1, -1],
        [0, -1, 1],
    ]
)
OPPOSITE = [0, 2, 1, 4, 3, 6, 5, 8, 7, 10, 9, 12, 11, 14, 13, 16, 15, 18, 17]
WEIGHTS = [1.0 / 3.0] + [1.0 / 18.0] * 6 + [1.0 / 36.0] * 12
relax_time = 0.9
vel_scale = 16.0


def extended(block, sides, width):
    for axis, dim in sides:
        count = lax.axis_size(axis)
        forward = [(i, i + 1) for i in range(count - 1)]
        forward.append((count - 1, 0))
        backward = [(target, source) for source, target in forward]
        low = lax.ppermute(
            lax.slice_in_dim(block, block.shape[dim] - width, None, axis=dim), axis, forward
        )
        high = lax.ppermute(lax.slice_in_dim(block, 0, width, axis=dim), axis, backward)
        block = jnp.concatenate([low, block, high], axis=dim)
    return block


def collide(populations, solid_flags, drag_rate):
    density = populations[0]
    for q in range(1, 19):
        density = density + populations[q]
    scale = 1.0 / (density * (1.0 + 0.5 * drag_rate))
    speeds = []
    for a in range(3):
        total = jnp.zeros_like(density)
        for q in range(19):
            if LATTICE[q, a] != 0:
                total = total + float(LATTICE[q, a]) * populations[q]
        speeds.append(total * scale)
    square = speeds[0] * speeds[0] + speeds[1] * speeds[1] + speeds[2] * speeds[2]
    relaxed = []
    for q in range(19):
        along = jnp.zeros_like(density)
        for a in range(3):
            if LATTICE[q, a] != 0:
                along = along + float(LATTICE[q, a]) * speeds[a]
        equilib = WEIGHTS[q] * density * (1.0 + 3.0 * along + 4.5 * along * along - 1.5 * square)
        relaxed.append(populations[q] - (populations[q] - equilib) / relax_time)
    relaxed = jnp.stack(relaxed)
    bounced = jnp.stack([populations[OPPOSITE[q]] for q in range(19)])
    result = jnp.where(solid_flags[None] == 1, bounced, relaxed)
    fluid_part = (1 - solid_flags).astype(jnp.float32)
    velocity = jnp.stack(speeds) * fluid_part[None]
    return (result, velocity)


def propagate(relaxed):
    padded = extended(relaxed, (("gx", 1), ("gy", 2), ("gz", 3)), 1)
    width_x, width_y, width_z = (relaxed.shape[1], relaxed.shape[2], relaxed.shape[3])
    moved = []
    for q in range(19):
        start_x = 1 - int(LATTICE[q, 0])
        start_y = 1 - int(LATTICE[q, 1])
        start_z = 1 - int(LATTICE[q, 2])
        moved.append(
            padded[
                q,
                start_x : start_x + width_x,
                start_y : start_y + width_y,
                start_z : start_z + width_z,
            ]
        )
    return jnp.stack(moved)


def on_device(pop_ratio, solid_flags, class_ids, drag_table, row_map, old_basis, old_sigma):
    weights = jnp.asarray(WEIGHTS, jnp.float32)
    populations = pop_ratio * weights[:, None, None, None]
    drag_rate = jnp.zeros(class_ids.shape, jnp.float32)
    for c in range(drag_table.shape[0]):
        drag_rate = drag_rate + jnp.where(class_ids == c, drag_table[c], 0.0)
    snaps = []
    for step in range(STEPS):
        relaxed, velocity = collide(populations, solid_flags, drag_rate)
        snaps.append(velocity.reshape(3, -1))
        populations = propagate(relaxed)
    values = jnp.concatenate(snaps, 0) * (vel_scale / VOX_ROW)
    cell_count = values.shape[1]
    rows_local = cell_count // VOX_ROW
    owners = lax.axis_size(("gy", "gz"))
    slab_rows = row_map.reshape(-1)
    term = jax.vmap(lambda v: jax.ops.segment_sum(v, slab_rows, num_segments=rows_local * owners))(
        values
    )
    snapshot = lax.psum_scatter(term, ("gy", "gz"), scatter_dimension=1, tiled=True)
    augmented = jnp.concatenate([old_sigma[:, None] * old_basis, snapshot], 0)
    total_rows = rows_local * lax.axis_size(("gx", "gy", "gz"))
    gram = jnp.dot(augmented, augmented.T, precision=lax.Precision.HIGHEST) / float(total_rows)
    total = lax.psum(gram, ("gx", "gy", "gz"))
    upper = jnp.linalg.cholesky(total).T
    new_basis = jax.scipy.linalg.solve_triangular(upper.T, augmented, lower=True)
    return (populations, new_basis, upper)


def solution(mesh):
    in_specs = (
        P(None, "gx", "gy", "gz"),
        P("gx", "gy", "gz"),
        P("gx", "gy", "gz"),
        P(),
        P("gx", "gy", "gz"),
        P(None, ("gx", "gy", "gz")),
        P(),
    )
    out_specs = (P(None, "gx", "gy", "gz"), P(None, ("gx", "gy", "gz")), P())
    return jax.shard_map(
        on_device, mesh=mesh, in_specs=in_specs, out_specs=out_specs, check_vma=False
    )
```

profile of v0, /device:TPU:0, one launch (start us, length us, event | category | flops | bytes accessed | tf_op | source)
XLA Modules:
  0.0 212.3 jit_solution(5937198158549665154)
XLA Ops:
  7.2 1.6 fusion.537
  8.8 1.1 broadcast_multiply_fusion
  9.9 0.7 broadcast_compare_fusion
  10.6 5.8 %constant_dynamic-update-slice_fusion.37 = (f32[19,2,16,128]{3,2,1,0:T(8,128)S(1)}, f32[2,16,128]{2,1,0:T(8,128)S(1)}, f32[2,16,128]{2,1,0:T(8,128)S(1)}, f32[2,...) fusion(f32[19,2,16,128]{3,2,1,0:T(8,128)S(1)} %broadcast_multiply_fus, ...), kind=kLoop, calls=%fused_computation.45 | loop fusion | flops 405503 | bytes 442400
  16.9 5.1 %collective-permute-start = (f32[19,1,16,128]{3,2,1,0:T(8,128)S(1)}, f32[19,1,16,128]{3,2,1,0:T(8,128)S(1)}, u32[]{:S(2)}, u32[]{:S(2)}) collective-permute-start(f32[19,1,16,128]{3,2,1,0:T(8,128)S(1)} %get-tuple-element.114), channel_id=1, source_target_pairs={{8,0},{16,8},{24,16},{0,24},{9,1},{17,9},{25,17},{1,25},{10,2},{18... | collective-permute-start | bytes 466952 | tf_op jit(solution)/shard_map/ppermute | solution.py:47
  22.1 4.4 %collective-permute-done = f32[19,1,16,128]{3,2,1,0:T(8,128)S(1)} collective-permute-done((f32[19,1,16,128]{3,2,1,0:T(8,128)S(1)}, f32[19,1,16,128]{3,2,1,0:T(8,128)S(1)}, u32[]{:S(2)}, u32[]{:S(2)}) %collective-permute-start) | collective-permute-done | bytes 155680 | tf_op jit(solution)/shard_map/ppermute | solution.py:47
  26.5 3.1 %collective-permute-done.1 = f32[19,1,16,128]{3,2,1,0:T(8,128)S(1)} collective-permute-done((f32[19,1,16,128]{3,2,1,0:T(8,128)S(1)}, f32[19,1,16,128]{3,2,1,0:T(8,128)S(1)}, u32[]{:S(2)}, u32[]{:S(2)}) %collective-permute-start.1) | collective-permute-done | bytes 155680 | tf_op jit(solution)/shard_map/ppermute | solution.py:44
  29.6 1.6 collective-permute-start.2
  31.7 2.0 collective-permute-done.2
  33.7 1.5 collective-permute-done.3
  35.7 0.6 copy.90
  36.3 0.6 copy.92
  36.9 0.5 collective-permute-start.5
  37.4 0.5 collective-permute-done.4
  37.9 1.0 copy.91
  39.0 1.3 collective-permute-done.5
  40.3 1.0 copy.93
  42.2 1.8 collective-permute-start.6
  44.2 4.3 %collective-permute-done.6 = f32[19,1,16,128]{3,2,1,0:T(8,128)S(1)} collective-permute-done((f32[19,1,16,128]{3,2,1,0:T(8,128)S(1)}, f32[19,1,16,128]{3,2,1,0:T(8,128)S(1)}, u32[]{:S(2)}, u32[]{:S(2)}) %collective-permute-start.6) | collective-permute-done | bytes 155680 | tf_op jit(solution)/shard_map/ppermute | solution.py:47
  48.5 3.6 %collective-permute-done.7 = f32[19,1,16,128]{3,2,1,0:T(8,128)S(1)} collective-permute-done((f32[19,1,16,128]{3,2,1,0:T(8,128)S(1)}, f32[19,1,16,128]{3,2,1,0:T(8,128)S(1)}, u32[]{:S(2)}, u32[]{:S(2)}) %collective-permute-start.7) | collective-permute-done | bytes 155680 | tf_op jit(solution)/shard_map/ppermute | solution.py:44
  52.1 0.6 collective-permute-start.8
  52.7 1.5 collective-permute-start.9
  54.2 2.0 collective-permute-done.8
  57.1 0.6 copy.94
  57.8 0.6 copy.96
  58.4 0.5 collective-permute-start.11
  58.9 0.5 collective-permute-done.10
  59.4 1.0 copy.95
  60.4 1.3 collective-permute-done.11
  61.8 1.0 copy.97
  63.7 2.3 %collective-permute-start.12 = (f32[19,1,16,128]{3,2,1,0:T(8,128)S(1)}, f32[19,1,16,128]{3,2,1,0:T(8,128)S(1)}, u32[]{:S(2)}, u32[]{:S(2)}) collective-permute-start(f32[19,1,16,128]{3,2,1,0:T(8,128)S(1)} %get-tuple-element.110), channel_id=1, source_target_pairs={{8,0},{16,8},{24,16},{0,24},{9,1},{17,9},{25,17},{1,25},{10,2},{18... | collective-permute-start | bytes 466952 | tf_op jit(solution)/shard_map/ppermute | solution.py:47
  66.1 4.3 %collective-permute-done.12 = f32[19,1,16,128]{3,2,1,0:T(8,128)S(1)} collective-permute-done((f32[19,1,16,128]{3,2,1,0:T(8,128)S(1)}, f32[19,1,16,128]{3,2,1,0:T(8,128)S(1)}, u32[]{:S(2)}, u32[]{:S(2)}) %collective-permute-start.12) | collective-permute-done | bytes 155680 | tf_op jit(solution)/shard_map/ppermute | solution.py:47
  70.4 3.7 %collective-permute-done.13 = f32[19,1,16,128]{3,2,1,0:T(8,128)S(1)} collective-permute-done((f32[19,1,16,128]{3,2,1,0:T(8,128)S(1)}, f32[19,1,16,128]{3,2,1,0:T(8,128)S(1)}, u32[]{:S(2)}, u32[]{:S(2)}) %collective-permute-start.13) | collective-permute-done | bytes 155680 | tf_op jit(solution)/shard_map/ppermute | solution.py:44
  74.2 1.6 collective-permute-start.14
  76.3 1.9 collective-permute-done.14
  78.2 1.5 collective-permute-done.15
  80.2 0.6 copy.98
  80.9 0.6 copy.100
  81.5 0.7 collective-permute-start.17
  82.5 1.1 copy.99
  83.6 1.5 collective-permute-done.17
  85.1 1.1 copy.101
  87.0 0.5 collective-permute-start.18
  87.5 3.3 %collective-permute-start.19 = (f32[19,1,16,128]{3,2,1,0:T(8,128)S(1)}, f32[19,1,16,128]{3,2,1,0:T(8,128)S(1)}, u32[]{:S(2)}, u32[]{:S(2)}) collective-permute-start(f32[19,1,16,128]{3,2,1,0:T(8,128)S(1)} %get-tuple-element.107), channel_id=1, source_target_pairs={{8,0},{16,8},{24,16},{0,24},{9,1},{17,9},{25,17},{1,25},{10,2},{18... | collective-permute-start | bytes 466952 | tf_op jit(solution)/shard_map/ppermute | solution.py:47
  91.1 0.6 copy.106
  91.8 23.9 %scatter_custom_fusion = f32[12,4096]{0,1:T(8,128)} fusion(s32[4096]{0:T(1024)} %bitcast.1436, f32[4096,12]{1,0:T(8,128)S(1)} %copy.106, f32[]{:T(128)} %constant.170.clone.1), kind=kCustom, calls=%fused_computation.2 | custom fusion | flops 49152 | bytes 197120 | tf_op jit(solution)/shard_map/vmap()/scatter-add | solution.py:116
  115.8 0.6 collective-permute-start.20
  116.4 1.5 collective-permute-start.21
  117.9 1.9 collective-permute-done.20
  120.8 0.7 copy.102
  121.5 0.7 copy.104
  122.2 1.7 collective-permute-start.23
  124.0 1.1 collective-permute-done.22
  125.0 0.6 copy.103
  125.7 0.6 copy.105
  127.1 27.1 %reduce-scatter.2.cloned.1.call-done = f32[12,512]{0,1:T(8,128)} async-done(((f32[12,4096]{0,1:T(8,128)}), f32[12,512]{0,1:T(8,128)}) %reduce-scatter.2.cloned.1.call-update) | async-done | bytes 24592 | tf_op jit(solution)/shard_map/reduce_scatter | solution.py:119
  154.2 1.1 copy.107
  155.5 39.5 %psum.7 = f32[44,44]{0,1:T(8,128)S(1)} all-reduce(f32[44,44]{0,1:T(8,128)S(1)} %convolution_multiply_fusion), channel_id=1, replica_groups=mesh['gx'=4,'gy'=2,'gz'=4] {'gx','gy','gz'}, use_global_device_ids=true, to_apply=%region_2.3 | all-reduce | flops 1936 | bytes 15488 | tf_op jit(solution)/shard_map/psum | solution.py:123
  195.1 4.0 %cholesky.16 = f32[44,44]{1,0:T(8,128)S(1)} custom-call(f32[44,44]{1,0:T(8,128)S(1)} %fusion.5), custom_call_target="Cholesky" | custom-call | tf_op jit(solution)/shard_map/jit(cholesky)/cholesky | solution.py:124
  199.2 0.6 compare_reduce_fusion
  199.8 0.7 fusion.6
  200.5 3.4 %custom-call.7 = f32[1,44,44]{1,2,0:T(8,128)S(1)} custom-call(f32[1,44,44]{2,1,0:T(8,128)S(1)} %get-tuple-element.152), custom_call_target="InvertDiagBlocksLowerTriangular" | custom-call | tf_op jit(solution)/shard_map/jit(_solve_triangular)/triangular_solve | solution.py:125
  203.9 0.9 fusion.3
  204.8 0.7 copy.110
  (177 shorter events, 8.8 us)
Async XLA Ops:
  7.2 147.1 %reduce-scatter.2.cloned.1.call-start = ((), (), s32[]{:S(2)}) async-start(), calls=%async_computation.1 | async-start | bytes 2359296 | tf_op jit(solution)/shard_map/reduce_scatter | solution.py:119
  16.9 9.5 %collective-permute-start = (f32[19,1,16,128]{3,2,1,0:T(8,128)S(1)}, f32[19,1,16,128]{3,2,1,0:T(8,128)S(1)}, u32[]{:S(2)}, u32[]{:S(2)}) collective-permute-start(f32[19,1,16,128]{3,2,1,0:T(8,128)S(1)} %get-tuple-element.114), channel_id=1, source_target_pairs={{8,0},{16,8},{24,16},{0,24},{9,1},{17,9},{25,17},{1,25},{10,2},{18... | collective-permute-start | bytes 466952 | tf_op jit(solution)/shard_map/ppermute | solution.py:47
  22.1 7.5 %collective-permute-start.1 = (f32[19,1,16,128]{3,2,1,0:T(8,128)S(1)}, f32[19,1,16,128]{3,2,1,0:T(8,128)S(1)}, u32[]{:S(2)}, u32[]{:S(2)}) collective-permute-start(f32[19,1,16,128]{3,2,1,0:T(8,128)S(1)} %get-tuple-element.113), channel_id=1, source_target_pairs={{0,8},{8,16},{16,24},{24,0},{1,9},{9,17},{17,25},{25,1},{2,10},{10... | collective-permute-start | bytes 466952 | tf_op jit(solution)/shard_map/ppermute | solution.py:44
  29.6 4.0 %collective-permute-start.2 = (f32[19,4,1,128]{3,2,1,0:T(1,128)S(1)}, f32[19,4,1,128]{3,2,1,0:T(1,128)S(1)}, u32[]{:S(2)}, u32[]{:S(2)}) collective-permute-start(f32[19,4,1,128]{3,2,1,0:T(1,128)S(1)} %get-tuple-element.106), channel_id=1, source_target_pairs={{4,0},{0,4},{5,1},{1,5},{6,2},{2,6},{7,3},{3,7},{12,8},{8,12},{13,... | collective-permute-start | bytes 116744 | tf_op jit(solution)/shard_map/ppermute | solution.py:47
  31.2 4.0 %collective-permute-start.3 = (f32[19,4,1,128]{3,2,1,0:T(1,128)S(1)}, f32[19,4,1,128]{3,2,1,0:T(1,128)S(1)}, u32[]{:S(2)}, u32[]{:S(2)}) collective-permute-start(f32[19,4,1,128]{3,2,1,0:T(1,128)S(1)} %get-tuple-element.105), channel_id=1, source_target_pairs={{0,4},{4,0},{1,5},{5,1},{2,6},{6,2},{3,7},{7,3},{8,12},{12,8},{9,1... | collective-permute-start | bytes 116744 | tf_op jit(solution)/shard_map/ppermute | solution.py:44
  36.3 1.7 collective-permute-start.4
  36.9 3.4 %collective-permute-start.5 = (f32[19,4,18,1]{0,1,3,2:T(4,128)S(1)}, f32[19,4,18,1]{0,1,3,2:T(4,128)S(1)}, u32[]{:S(2)}, u32[]{:S(2)}) collective-permute-start(f32[19,4,18,1]{0,1,3,2:T(4,128)S(1)} %copy.92), channel_id=1, source_target_pairs={{0,1},{1,2},{2,3},{3,0},{4,5},{5,6},{6,7},{7,4},{8,9},{9,10},{10,1... | collective-permute-start | bytes 16424 | tf_op jit(solution)/shard_map/ppermute | solution.py:44
  42.2 6.3 %collective-permute-start.6 = (f32[19,1,16,128]{3,2,1,0:T(8,128)S(1)}, f32[19,1,16,128]{3,2,1,0:T(8,128)S(1)}, u32[]{:S(2)}, u32[]{:S(2)}) collective-permute-start(f32[19,1,16,128]{3,2,1,0:T(8,128)S(1)} %get-tuple-element.112), channel_id=1, source_target_pairs={{8,0},{16,8},{24,16},{0,24},{9,1},{17,9},{25,17},{1,25},{10,2},{18... | collective-permute-start | bytes 466952 | tf_op jit(solution)/shard_map/ppermute | solution.py:47
  44.0 8.1 %collective-permute-start.7 = (f32[19,1,16,128]{3,2,1,0:T(8,128)S(1)}, f32[19,1,16,128]{3,2,1,0:T(8,128)S(1)}, u32[]{:S(2)}, u32[]{:S(2)}) collective-permute-start(f32[19,1,16,128]{3,2,1,0:T(8,128)S(1)} %get-tuple-element.111), channel_id=1, source_target_pairs={{0,8},{8,16},{16,24},{24,0},{1,9},{9,17},{17,25},{25,1},{2,10},{10... | collective-permute-start | bytes 466952 | tf_op jit(solution)/shard_map/ppermute | solution.py:44
  52.1 4.0 %collective-permute-start.8 = (f32[19,4,1,128]{3,2,1,0:T(1,128)S(1)}, f32[19,4,1,128]{3,2,1,0:T(1,128)S(1)}, u32[]{:S(2)}, u32[]{:S(2)}) collective-permute-start(f32[19,4,1,128]{3,2,1,0:T(1,128)S(1)} %get-tuple-element.104), channel_id=1, source_target_pairs={{4,0},{0,4},{5,1},{1,5},{6,2},{2,6},{7,3},{3,7},{12,8},{8,12},{13,... | collective-permute-start | bytes 116744 | tf_op jit(solution)/shard_map/ppermute | solution.py:47
  52.7 4.0 %collective-permute-start.9 = (f32[19,4,1,128]{3,2,1,0:T(1,128)S(1)}, f32[19,4,1,128]{3,2,1,0:T(1,128)S(1)}, u32[]{:S(2)}, u32[]{:S(2)}) collective-permute-start(f32[19,4,1,128]{3,2,1,0:T(1,128)S(1)} %get-tuple-element.103), channel_id=1, source_target_pairs={{0,4},{4,0},{1,5},{5,1},{2,6},{6,2},{3,7},{7,3},{8,12},{12,8},{9,1... | collective-permute-start | bytes 116744 | tf_op jit(solution)/shard_map/ppermute | solution.py:44
  57.7 1.7 collective-permute-start.10
  58.4 3.4 %collective-permute-start.11 = (f32[19,4,18,1]{0,1,3,2:T(4,128)S(1)}, f32[19,4,18,1]{0,1,3,2:T(4,128)S(1)}, u32[]{:S(2)}, u32[]{:S(2)}) collective-permute-start(f32[19,4,18,1]{0,1,3,2:T(4,128)S(1)} %copy.96), channel_id=1, source_target_pairs={{0,1},{1,2},{2,3},{3,0},{4,5},{5,6},{6,7},{7,4},{8,9},{9,10},{10,1... | collective-permute-start | bytes 16424 | tf_op jit(solution)/shard_map/ppermute | solution.py:44
  63.0 3.0 %copy-start.1 = (f32[32,512]{1,0:T(8,128)S(1)}, f32[32,512]{1,0:T(8,128)}, u32[]{:S(2)}) copy-start(f32[32,512]{1,0:T(8,128)} %param.13) | copy-start | bytes 196612
  63.0 2.9 %copy-start.3 = (f32[32]{0:T(128)S(1)}, f32[32]{0:T(128)}, u32[]{:S(2)}) copy-start(f32[32]{0:T(128)} %param.14) | copy-start | bytes 388
  63.1 13.1 %copy-start = (s32[2,16,128]{2,1,0:T(8,128)S(1)}, s32[2,16,128]{2,1,0:T(8,128)}, u32[]{:S(2)}) copy-start(s32[2,16,128]{2,1,0:T(8,128)} %param.9) | copy-start | bytes 49156
  63.7 6.7 %collective-permute-start.12 = (f32[19,1,16,128]{3,2,1,0:T(8,128)S(1)}, f32[19,1,16,128]{3,2,1,0:T(8,128)S(1)}, u32[]{:S(2)}, u32[]{:S(2)}) collective-permute-start(f32[19,1,16,128]{3,2,1,0:T(8,128)S(1)} %get-tuple-element.110), channel_id=1, source_target_pairs={{8,0},{16,8},{24,16},{0,24},{9,1},{17,9},{25,17},{1,25},{10,2},{18... | collective-permute-start | bytes 466952 | tf_op jit(solution)/shard_map/ppermute | solution.py:47
  66.0 8.2 %collective-permute-start.13 = (f32[19,1,16,128]{3,2,1,0:T(8,128)S(1)}, f32[19,1,16,128]{3,2,1,0:T(8,128)S(1)}, u32[]{:S(2)}, u32[]{:S(2)}) collective-permute-start(f32[19,1,16,128]{3,2,1,0:T(8,128)S(1)} %get-tuple-element.109), channel_id=1, source_target_pairs={{0,8},{8,16},{16,24},{24,0},{1,9},{9,17},{17,25},{25,1},{2,10},{10... | collective-permute-start | bytes 466952 | tf_op jit(solution)/shard_map/ppermute | solution.py:44
  74.2 4.0 %collective-permute-start.14 = (f32[19,4,1,128]{3,2,1,0:T(1,128)S(1)}, f32[19,4,1,128]{3,2,1,0:T(1,128)S(1)}, u32[]{:S(2)}, u32[]{:S(2)}) collective-permute-start(f32[19,4,1,128]{3,2,1,0:T(1,128)S(1)} %get-tuple-element.102), channel_id=1, source_target_pairs={{4,0},{0,4},{5,1},{1,5},{6,2},{2,6},{7,3},{3,7},{12,8},{8,12},{13,... | collective-permute-start | bytes 116744 | tf_op jit(solution)/shard_map/ppermute | solution.py:47
  75.8 4.0 %collective-permute-start.15 = (f32[19,4,1,128]{3,2,1,0:T(1,128)S(1)}, f32[19,4,1,128]{3,2,1,0:T(1,128)S(1)}, u32[]{:S(2)}, u32[]{:S(2)}) collective-permute-start(f32[19,4,1,128]{3,2,1,0:T(1,128)S(1)} %get-tuple-element.101), channel_id=1, source_target_pairs={{0,4},{4,0},{1,5},{5,1},{2,6},{6,2},{3,7},{7,3},{8,12},{12,8},{9,1... | collective-permute-start | bytes 116744 | tf_op jit(solution)/shard_map/ppermute | solution.py:44
  80.8 1.7 collective-permute-start.16
  81.5 3.6 %collective-permute-start.17 = (f32[19,4,18,1]{0,1,3,2:T(4,128)S(1)}, f32[19,4,18,1]{0,1,3,2:T(4,128)S(1)}, u32[]{:S(2)}, u32[]{:S(2)}) collective-permute-start(f32[19,4,18,1]{0,1,3,2:T(4,128)S(1)} %copy.100), channel_id=1, source_target_pairs={{0,1},{1,2},{2,3},{3,0},{4,5},{5,6},{6,7},{7,4},{8,9},{9,10},{10,1... | collective-permute-start | bytes 16424 | tf_op jit(solution)/shard_map/ppermute | solution.py:44
  87.0 28.7 %collective-permute-start.18 = (f32[19,1,16,128]{3,2,1,0:T(8,128)S(1)}, f32[19,1,16,128]{3,2,1,0:T(8,128)S(1)}, u32[]{:S(2)}, u32[]{:S(2)}) collective-permute-start(f32[19,1,16,128]{3,2,1,0:T(8,128)S(1)} %get-tuple-element.108), channel_id=1, source_target_pairs={{0,8},{8,16},{16,24},{24,0},{1,9},{9,17},{17,25},{25,1},{2,10},{10... | collective-permute-start | bytes 466952 | tf_op jit(solution)/shard_map/ppermute | solution.py:44
  87.5 28.2 %collective-permute-start.19 = (f32[19,1,16,128]{3,2,1,0:T(8,128)S(1)}, f32[19,1,16,128]{3,2,1,0:T(8,128)S(1)}, u32[]{:S(2)}, u32[]{:S(2)}) collective-permute-start(f32[19,1,16,128]{3,2,1,0:T(8,128)S(1)} %get-tuple-element.107), channel_id=1, source_target_pairs={{8,0},{16,8},{24,16},{0,24},{9,1},{17,9},{25,17},{1,25},{10,2},{18... | collective-permute-start | bytes 466952 | tf_op jit(solution)/shard_map/ppermute | solution.py:47
  115.8 4.0 %collective-permute-start.20 = (f32[19,4,1,128]{3,2,1,0:T(1,128)S(1)}, f32[19,4,1,128]{3,2,1,0:T(1,128)S(1)}, u32[]{:S(2)}, u32[]{:S(2)}) collective-permute-start(f32[19,4,1,128]{3,2,1,0:T(1,128)S(1)} %get-tuple-element.100), channel_id=1, source_target_pairs={{0,4},{4,0},{1,5},{5,1},{2,6},{6,2},{3,7},{7,3},{8,12},{12,8},{9,1... | collective-permute-start | bytes 116744 | tf_op jit(solution)/shard_map/ppermute | solution.py:44
  116.4 4.0 %collective-permute-start.21 = (f32[19,4,1,128]{3,2,1,0:T(1,128)S(1)}, f32[19,4,1,128]{3,2,1,0:T(1,128)S(1)}, u32[]{:S(2)}, u32[]{:S(2)}) collective-permute-start(f32[19,4,1,128]{3,2,1,0:T(1,128)S(1)} %get-tuple-element.99), channel_id=1, source_target_pairs={{4,0},{0,4},{5,1},{1,5},{6,2},{2,6},{7,3},{3,7},{12,8},{8,12},{13,... | collective-permute-start | bytes 116744 | tf_op jit(solution)/shard_map/ppermute | solution.py:47
  121.5 3.5 %collective-permute-start.22 = (f32[19,4,18,1]{2,0,3,1:T(8,128)S(1)}, f32[19,4,18,1]{2,0,3,1:T(8,128)S(1)}, u32[]{:S(2)}, u32[]{:S(2)}) collective-permute-start(f32[19,4,18,1]{2,0,3,1:T(8,128)S(1)} %copy.102), channel_id=1, source_target_pairs={{0,1},{1,2},{2,3},{3,0},{4,5},{5,6},{6,7},{7,4},{8,9},{9,10},{10,1... | collective-permute-start | bytes 16424 | tf_op jit(solution)/shard_map/ppermute | solution.py:44
  122.2 3.5 %collective-permute-start.23 = (f32[19,4,18,1]{2,0,3,1:T(8,128)S(1)}, f32[19,4,18,1]{2,0,3,1:T(8,128)S(1)}, u32[]{:S(2)}, u32[]{:S(2)}) collective-permute-start(f32[19,4,18,1]{2,0,3,1:T(8,128)S(1)} %copy.104), channel_id=1, source_target_pairs={{1,0},{2,1},{3,2},{0,3},{5,4},{6,5},{7,6},{4,7},{9,8},{10,9},{11,1... | collective-permute-start | bytes 16424 | tf_op jit(solution)/shard_map/ppermute | solution.py:47
  127.1 78.4 %copy-start.2 = (f32[19,2,16,128]{3,2,1,0:T(8,128)}, f32[19,2,16,128]{3,2,1,0:T(8,128)S(1)}, u32[]{:S(2)}) copy-start(f32[19,2,16,128]{3,2,1,0:T(8,128)S(1)} %constant_dynamic-update-slice_fusion.152) | copy-start | bytes 933892
Sparse Core Ops, SparseCore 0:
  115.8 38.3 reduce-scatter.1
where the time goes:
time: 213 us; the launch traced here: 212 us
  waiting for transfers between devices  69 us (32%)
  other arithmetic  44.2 us (21%)
  blocking collectives  39.5 us (19%)
  starting transfers between devices  25.4 us (12%)
  local copies, waits for them, and re-layouts  18 us (8%)
  between operations  15 us (7%)
    psum x1, blocking collectives, on_device(): total = lax.psum(gram, ('gx', 'gy', 'gz'))  39.5 us
    reduce_scatter x1, waiting for transfers between devices, on_device(): lax.psum_scatter(term, ('gy', 'gz'), scatter_dimension=1, tiled=True)  27.1 us
    scatter-add x1, other arithmetic, on_device(): jax.ops.segment_sum(v, slab_rows, num_segments=rows_local * owners)  23.9 us
    ppermute x12, waiting for transfers between devices, extended(): lax.ppermute(lax.slice_in_dim(block, block.shape[dim] - width, None, axis...  21.1 us
    ppermute x12, waiting for transfers between devices, extended(): lax.ppermute(lax.slice_in_dim(block, 0, width, axis=dim), axis, backward)  20.8 us
    ppermute x12, starting transfers between devices, extended(): lax.ppermute(lax.slice_in_dim(block, 0, width, axis=dim), axis, backward)  19.7 us
    unnamed x89, other arithmetic  8.3 us
    ppermute x12, starting transfers between devices, extended(): lax.ppermute(lax.slice_in_dim(block, block.shape[dim] - width, None, axis...  5.69 us
  transfers between devices with their start and end apart: 25, of which 23 were waited for; matrix products, arithmetic and copies ran while one was open for 16% of the time, Pallas kernels for 0%

commit v1 on v0

--- a/solution.py
+++ b/solution.py
@@ -1,3 +1,4 @@
+import functools
 import jax
 import jax.numpy as jnp
 import numpy as np
@@ -33,6 +34,13 @@
 WEIGHTS = [1.0 / 3.0] + [1.0 / 18.0] * 6 + [1.0 / 36.0] * 12
 relax_time = 0.9
 vel_scale = 16.0
+
+
+def save_the_ways(mat, axis_key):
+    return lax.all_gather(mat, axis_key).sum(axis=0)
+
+
+proceed_patches = functools.partial(save_the_ways, axis_key=("gx", "gy", "gz"))
 
 
 def extended(block, sides, width):
@@ -120,7 +128,7 @@
     augmented = jnp.concatenate([old_sigma[:, None] * old_basis, snapshot], 0)
     total_rows = rows_local * lax.axis_size(("gx", "gy", "gz"))
     gram = jnp.dot(augmented, augmented.T, precision=lax.Precision.HIGHEST) / float(total_rows)
-    total = lax.psum(gram, ("gx", "gy", "gz"))
+    total = proceed_patches(gram)
     upper = jnp.linalg.cholesky(total).T
     new_basis = jax.scipy.linalg.solve_triangular(upper.T, augmented, lower=True)
     return (populations, new_basis, upper)

time: 213 us -> 216 us (1.014)
  blocking collectives: 39.5 us -> 42.7 us
    all_gather x0 -> x1, blocking collectives: none -> 42.7 us  [save_the_ways(): return lax.all_gather(mat, axis_key).sum(axis=0)]
    psum x1 -> x0, blocking collectives: 39.5 us -> none  [on_device(): total = lax.psum(gram, ('gx', 'gy', 'gz'))]
where the time goes in v1:
time: 216 us
  waiting for transfers between devices  69 us (32%)
  other arithmetic  44.3 us (21%)
  blocking collectives  42.7 us (20%)
  starting transfers between devices  25.4 us (12%)
  local copies, waits for them, and re-layouts  18 us (8%)
  between operations  15 us (7%)
    all_gather x1, blocking collectives, save_the_ways(): return lax.all_gather(mat, axis_key).sum(axis=0)  42.7 us
    reduce_scatter x1, waiting for transfers between devices, on_device(): lax.psum_scatter(term, ('gy', 'gz'), scatter_dimension=1, tiled=True)  27.1 us
    scatter-add x1, other arithmetic, on_device(): jax.ops.segment_sum(v, slab_rows, num_segments=rows_local * owners)  23.9 us
    ppermute x12, waiting for transfers between devices, extended(): lax.ppermute(lax.slice_in_dim(block, block.shape[dim] - width, None, axis...  21.1 us
    ppermute x12, waiting for transfers between devices, extended(): lax.ppermute(lax.slice_in_dim(block, 0, width, axis=dim), axis, backward)  20.8 us
    ppermute x12, starting transfers between devices, extended(): lax.ppermute(lax.slice_in_dim(block, 0, width, axis=dim), axis, backward)  19.7 us
    unnamed x89, other arithmetic  8.3 us
    ppermute x12, starting transfers between devices, extended(): lax.ppermute(lax.slice_in_dim(block, block.shape[dim] - width, None, axis...  5.69 us
  transfers between devices with their start and end apart: 25, of which 23 were waited for; matrix products, arithmetic and copies ran while one was open for 16% of the time, Pallas kernels for 0%

profile of v1, /device:TPU:0, one launch (start us, length us, event | category | flops | bytes accessed | tf_op | source)
XLA Modules:
  0.0 215.6 jit_solution(13114048192198215583)
XLA Ops:
  7.2 1.6 fusion.538
  8.8 1.1 broadcast_multiply_fusion
  9.9 0.7 broadcast_compare_fusion
  10.6 5.8 %constant_dynamic-update-slice_fusion.37 = (f32[19,2,16,128]{3,2,1,0:T(8,128)S(1)}, f32[2,16,128]{2,1,0:T(8,128)S(1)}, f32[2,16,128]{2,1,0:T(8,128)S(1)}, f32[2,...) fusion(f32[19,2,16,128]{3,2,1,0:T(8,128)S(1)} %broadcast_multiply_fus, ...), kind=kLoop, calls=%fused_computation.46 | loop fusion | flops 405503 | bytes 442400
  16.9 5.1 %collective-permute-start = (f32[19,1,16,128]{3,2,1,0:T(8,128)S(1)}, f32[19,1,16,128]{3,2,1,0:T(8,128)S(1)}, u32[]{:S(2)}, u32[]{:S(2)}) collective-permute-start(f32[19,1,16,128]{3,2,1,0:T(8,128)S(1)} %get-tuple-element.114), channel_id=1, source_target_pairs={{8,0},{16,8},{24,16},{0,24},{9,1},{17,9},{25,17},{1,25},{10,2},{18... | collective-permute-start | bytes 466952 | tf_op jit(solution)/shard_map/ppermute | solution.py:55
  22.1 4.4 %collective-permute-done = f32[19,1,16,128]{3,2,1,0:T(8,128)S(1)} collective-permute-done((f32[19,1,16,128]{3,2,1,0:T(8,128)S(1)}, f32[19,1,16,128]{3,2,1,0:T(8,128)S(1)}, u32[]{:S(2)}, u32[]{:S(2)}) %collective-permute-start) | collective-permute-done | bytes 155680 | tf_op jit(solution)/shard_map/ppermute | solution.py:55
  26.5 3.1 %collective-permute-done.1 = f32[19,1,16,128]{3,2,1,0:T(8,128)S(1)} collective-permute-done((f32[19,1,16,128]{3,2,1,0:T(8,128)S(1)}, f32[19,1,16,128]{3,2,1,0:T(8,128)S(1)}, u32[]{:S(2)}, u32[]{:S(2)}) %collective-permute-start.1) | collective-permute-done | bytes 155680 | tf_op jit(solution)/shard_map/ppermute | solution.py:52
  29.6 1.6 collective-permute-start.2
  31.7 2.0 collective-permute-done.2
  33.7 1.5 collective-permute-done.3
  35.7 0.6 copy.88
  36.3 0.6 copy.90
  36.9 0.5 collective-permute-start.5
  37.4 0.5 collective-permute-done.4
  37.9 1.0 copy.89
  39.0 1.3 collective-permute-done.5
  40.3 1.0 copy.91
  42.2 1.8 collective-permute-start.6
  44.2 4.3 %collective-permute-done.6 = f32[19,1,16,128]{3,2,1,0:T(8,128)S(1)} collective-permute-done((f32[19,1,16,128]{3,2,1,0:T(8,128)S(1)}, f32[19,1,16,128]{3,2,1,0:T(8,128)S(1)}, u32[]{:S(2)}, u32[]{:S(2)}) %collective-permute-start.6) | collective-permute-done | bytes 155680 | tf_op jit(solution)/shard_map/ppermute | solution.py:55
  48.5 3.6 %collective-permute-done.7 = f32[19,1,16,128]{3,2,1,0:T(8,128)S(1)} collective-permute-done((f32[19,1,16,128]{3,2,1,0:T(8,128)S(1)}, f32[19,1,16,128]{3,2,1,0:T(8,128)S(1)}, u32[]{:S(2)}, u32[]{:S(2)}) %collective-permute-start.7) | collective-permute-done | bytes 155680 | tf_op jit(solution)/shard_map/ppermute | solution.py:52
  52.1 0.6 collective-permute-start.8
  52.7 1.5 collective-permute-start.9
  54.2 2.0 collective-permute-done.8
  57.1 0.6 copy.92
  57.8 0.6 copy.94
  58.4 0.5 collective-permute-start.11
  58.9 0.5 collective-permute-done.10
  59.4 1.0 copy.93
  60.4 1.3 collective-permute-done.11
  61.8 1.0 copy.95
  63.7 2.3 %collective-permute-start.12 = (f32[19,1,16,128]{3,2,1,0:T(8,128)S(1)}, f32[19,1,16,128]{3,2,1,0:T(8,128)S(1)}, u32[]{:S(2)}, u32[]{:S(2)}) collective-permute-start(f32[19,1,16,128]{3,2,1,0:T(8,128)S(1)} %get-tuple-element.110), channel_id=1, source_target_pairs={{8,0},{16,8},{24,16},{0,24},{9,1},{17,9},{25,17},{1,25},{10,2},{18... | collective-permute-start | bytes 466952 | tf_op jit(solution)/shard_map/ppermute | solution.py:55
  66.1 4.3 %collective-permute-done.12 = f32[19,1,16,128]{3,2,1,0:T(8,128)S(1)} collective-permute-done((f32[19,1,16,128]{3,2,1,0:T(8,128)S(1)}, f32[19,1,16,128]{3,2,1,0:T(8,128)S(1)}, u32[]{:S(2)}, u32[]{:S(2)}) %collective-permute-start.12) | collective-permute-done | bytes 155680 | tf_op jit(solution)/shard_map/ppermute | solution.py:55
  70.4 3.7 %collective-permute-done.13 = f32[19,1,16,128]{3,2,1,0:T(8,128)S(1)} collective-permute-done((f32[19,1,16,128]{3,2,1,0:T(8,128)S(1)}, f32[19,1,16,128]{3,2,1,0:T(8,128)S(1)}, u32[]{:S(2)}, u32[]{:S(2)}) %collective-permute-start.13) | collective-permute-done | bytes 155680 | tf_op jit(solution)/shard_map/ppermute | solution.py:52
  74.2 1.6 collective-permute-start.14
  76.3 1.9 collective-permute-done.14
  78.2 1.5 collective-permute-done.15
  80.2 0.6 copy.96
  80.9 0.6 copy.98
  81.5 0.7 collective-permute-start.17
  82.5 1.1 copy.97
  83.6 1.5 collective-permute-done.17
  85.1 1.1 copy.99
  87.0 0.5 collective-permute-start.18
  87.5 3.3 %collective-permute-start.19 = (f32[19,1,16,128]{3,2,1,0:T(8,128)S(1)}, f32[19,1,16,128]{3,2,1,0:T(8,128)S(1)}, u32[]{:S(2)}, u32[]{:S(2)}) collective-permute-start(f32[19,1,16,128]{3,2,1,0:T(8,128)S(1)} %get-tuple-element.107), channel_id=1, source_target_pairs={{8,0},{16,8},{24,16},{0,24},{9,1},{17,9},{25,17},{1,25},{10,2},{18... | collective-permute-start | bytes 466952 | tf_op jit(solution)/shard_map/ppermute | solution.py:55
  91.1 0.6 copy.104
  91.8 23.9 %scatter_custom_fusion = f32[12,4096]{0,1:T(8,128)} fusion(s32[4096]{0:T(1024)} %bitcast.1438, f32[4096,12]{1,0:T(8,128)S(1)} %copy.104, f32[]{:T(128)} %constant.170.clone.1), kind=kCustom, calls=%fused_computation.3 | custom fusion | flops 49152 | bytes 197120 | tf_op jit(solution)/shard_map/vmap()/scatter-add | solution.py:124
  115.8 0.6 collective-permute-start.20
  116.4 1.5 collective-permute-start.21
  117.9 1.9 collective-permute-done.20
  120.8 0.7 copy.100
  121.5 0.7 copy.102
  122.2 1.7 collective-permute-start.23
  124.0 1.1 collective-permute-done.22
  125.0 0.6 copy.101
  125.7 0.6 copy.103
  127.1 27.1 %reduce-scatter.2.cloned.1.call-done = f32[12,512]{0,1:T(8,128)} async-done(((f32[12,4096]{0,1:T(8,128)}), f32[12,512]{0,1:T(8,128)}) %reduce-scatter.2.cloned.1.call-update) | async-done | bytes 24592 | tf_op jit(solution)/shard_map/reduce_scatter | solution.py:127
  154.2 1.1 copy.105
  155.5 42.7 %all-gather.1 = f32[32,44,44]{2,1,0:T(8,128)S(1)} all-gather(f32[1,44,44]{2,1,0:T(8,128)S(1)} %fusion), channel_id=2, replica_groups=mesh['gx'=4,'gy'=2,'gz'=4] {'gx','gy','gz'}, dimensions={0}, use_global_device_ids=true | all-gather | bytes 255552 | tf_op jit(solution)/shard_map/all_gather | solution.py:40
  198.4 4.0 %cholesky.16 = f32[44,44]{1,0:T(8,128)S(1)} custom-call(f32[44,44]{1,0:T(8,128)S(1)} %fusion.6), custom_call_target="Cholesky" | custom-call | tf_op jit(solution)/shard_map/jit(cholesky)/cholesky | solution.py:132
  202.4 0.6 compare_reduce_fusion
  203.1 0.7 fusion.7
  203.7 3.4 %custom-call.7 = f32[1,44,44]{1,2,0:T(8,128)S(1)} custom-call(f32[1,44,44]{2,1,0:T(8,128)S(1)} %get-tuple-element.152), custom_call_target="InvertDiagBlocksLowerTriangular" | custom-call | tf_op jit(solution)/shard_map/jit(_solve_triangular)/triangular_solve | solution.py:133
  207.1 0.9 fusion.4
  208.0 0.7 copy.107
  (178 shorter events, 8.9 us)
Async XLA Ops:
  7.2 147.1 %reduce-scatter.2.cloned.1.call-start = ((), (), s32[]{:S(2)}) async-start(), calls=%async_computation.1 | async-start | bytes 2359296 | tf_op jit(solution)/shard_map/reduce_scatter | solution.py:127
  16.9 9.5 %collective-permute-start = (f32[19,1,16,128]{3,2,1,0:T(8,128)S(1)}, f32[19,1,16,128]{3,2,1,0:T(8,128)S(1)}, u32[]{:S(2)}, u32[]{:S(2)}) collective-permute-start(f32[19,1,16,128]{3,2,1,0:T(8,128)S(1)} %get-tuple-element.114), channel_id=1, source_target_pairs={{8,0},{16,8},{24,16},{0,24},{9,1},{17,9},{25,17},{1,25},{10,2},{18... | collective-permute-start | bytes 466952 | tf_op jit(solution)/shard_map/ppermute | solution.py:55
  22.1 7.5 %collective-permute-start.1 = (f32[19,1,16,128]{3,2,1,0:T(8,128)S(1)}, f32[19,1,16,128]{3,2,1,0:T(8,128)S(1)}, u32[]{:S(2)}, u32[]{:S(2)}) collective-permute-start(f32[19,1,16,128]{3,2,1,0:T(8,128)S(1)} %get-tuple-element.113), channel_id=1, source_target_pairs={{0,8},{8,16},{16,24},{24,0},{1,9},{9,17},{17,25},{25,1},{2,10},{10... | collective-permute-start | bytes 466952 | tf_op jit(solution)/shard_map/ppermute | solution.py:52
  29.6 4.0 %collective-permute-start.2 = (f32[19,4,1,128]{3,2,1,0:T(1,128)S(1)}, f32[19,4,1,128]{3,2,1,0:T(1,128)S(1)}, u32[]{:S(2)}, u32[]{:S(2)}) collective-permute-start(f32[19,4,1,128]{3,2,1,0:T(1,128)S(1)} %get-tuple-element.106), channel_id=1, source_target_pairs={{4,0},{0,4},{5,1},{1,5},{6,2},{2,6},{7,3},{3,7},{12,8},{8,12},{13,... | collective-permute-start | bytes 116744 | tf_op jit(solution)/shard_map/ppermute | solution.py:55
  31.2 4.0 %collective-permute-start.3 = (f32[19,4,1,128]{3,2,1,0:T(1,128)S(1)}, f32[19,4,1,128]{3,2,1,0:T(1,128)S(1)}, u32[]{:S(2)}, u32[]{:S(2)}) collective-permute-start(f32[19,4,1,128]{3,2,1,0:T(1,128)S(1)} %get-tuple-element.105), channel_id=1, source_target_pairs={{0,4},{4,0},{1,5},{5,1},{2,6},{6,2},{3,7},{7,3},{8,12},{12,8},{9,1... | collective-permute-start | bytes 116744 | tf_op jit(solution)/shard_map/ppermute | solution.py:52
  36.3 1.7 collective-permute-start.4
  36.9 3.4 %collective-permute-start.5 = (f32[19,4,18,1]{0,1,3,2:T(4,128)S(1)}, f32[19,4,18,1]{0,1,3,2:T(4,128)S(1)}, u32[]{:S(2)}, u32[]{:S(2)}) collective-permute-start(f32[19,4,18,1]{0,1,3,2:T(4,128)S(1)} %copy.90), channel_id=1, source_target_pairs={{0,1},{1,2},{2,3},{3,0},{4,5},{5,6},{6,7},{7,4},{8,9},{9,10},{10,1... | collective-permute-start | bytes 16424 | tf_op jit(solution)/shard_map/ppermute | solution.py:52
  42.2 6.3 %collective-permute-start.6 = (f32[19,1,16,128]{3,2,1,0:T(8,128)S(1)}, f32[19,1,16,128]{3,2,1,0:T(8,128)S(1)}, u32[]{:S(2)}, u32[]{:S(2)}) collective-permute-start(f32[19,1,16,128]{3,2,1,0:T(8,128)S(1)} %get-tuple-element.112), channel_id=1, source_target_pairs={{8,0},{16,8},{24,16},{0,24},{9,1},{17,9},{25,17},{1,25},{10,2},{18... | collective-permute-start | bytes 466952 | tf_op jit(solution)/shard_map/ppermute | solution.py:55
  44.0 8.1 %collective-permute-start.7 = (f32[19,1,16,128]{3,2,1,0:T(8,128)S(1)}, f32[19,1,16,128]{3,2,1,0:T(8,128)S(1)}, u32[]{:S(2)}, u32[]{:S(2)}) collective-permute-start(f32[19,1,16,128]{3,2,1,0:T(8,128)S(1)} %get-tuple-element.111), channel_id=1, source_target_pairs={{0,8},{8,16},{16,24},{24,0},{1,9},{9,17},{17,25},{25,1},{2,10},{10... | collective-permute-start | bytes 466952 | tf_op jit(solution)/shard_map/ppermute | solution.py:52
  52.1 4.0 %collective-permute-start.8 = (f32[19,4,1,128]{3,2,1,0:T(1,128)S(1)}, f32[19,4,1,128]{3,2,1,0:T(1,128)S(1)}, u32[]{:S(2)}, u32[]{:S(2)}) collective-permute-start(f32[19,4,1,128]{3,2,1,0:T(1,128)S(1)} %get-tuple-element.104), channel_id=1, source_target_pairs={{4,0},{0,4},{5,1},{1,5},{6,2},{2,6},{7,3},{3,7},{12,8},{8,12},{13,... | collective-permute-start | bytes 116744 | tf_op jit(solution)/shard_map/ppermute | solution.py:55
  52.7 4.0 %collective-permute-start.9 = (f32[19,4,1,128]{3,2,1,0:T(1,128)S(1)}, f32[19,4,1,128]{3,2,1,0:T(1,128)S(1)}, u32[]{:S(2)}, u32[]{:S(2)}) collective-permute-start(f32[19,4,1,128]{3,2,1,0:T(1,128)S(1)} %get-tuple-element.103), channel_id=1, source_target_pairs={{0,4},{4,0},{1,5},{5,1},{2,6},{6,2},{3,7},{7,3},{8,12},{12,8},{9,1... | collective-permute-start | bytes 116744 | tf_op jit(solution)/shard_map/ppermute | solution.py:52
  57.7 1.7 collective-permute-start.10
  58.4 3.4 %collective-permute-start.11 = (f32[19,4,18,1]{0,1,3,2:T(4,128)S(1)}, f32[19,4,18,1]{0,1,3,2:T(4,128)S(1)}, u32[]{:S(2)}, u32[]{:S(2)}) collective-permute-start(f32[19,4,18,1]{0,1,3,2:T(4,128)S(1)} %copy.94), channel_id=1, source_target_pairs={{0,1},{1,2},{2,3},{3,0},{4,5},{5,6},{6,7},{7,4},{8,9},{9,10},{10,1... | collective-permute-start | bytes 16424 | tf_op jit(solution)/shard_map/ppermute | solution.py:52
  63.0 3.0 %copy-start.1 = (f32[32,512]{1,0:T(8,128)S(1)}, f32[32,512]{1,0:T(8,128)}, u32[]{:S(2)}) copy-start(f32[32,512]{1,0:T(8,128)} %param.13) | copy-start | bytes 196612
  63.0 2.9 %copy-start.3 = (f32[32]{0:T(128)S(1)}, f32[32]{0:T(128)}, u32[]{:S(2)}) copy-start(f32[32]{0:T(128)} %param.14) | copy-start | bytes 388
  63.1 13.1 %copy-start = (s32[2,16,128]{2,1,0:T(8,128)S(1)}, s32[2,16,128]{2,1,0:T(8,128)}, u32[]{:S(2)}) copy-start(s32[2,16,128]{2,1,0:T(8,128)} %param.9) | copy-start | bytes 49156
  63.7 6.7 %collective-permute-start.12 = (f32[19,1,16,128]{3,2,1,0:T(8,128)S(1)}, f32[19,1,16,128]{3,2,1,0:T(8,128)S(1)}, u32[]{:S(2)}, u32[]{:S(2)}) collective-permute-start(f32[19,1,16,128]{3,2,1,0:T(8,128)S(1)} %get-tuple-element.110), channel_id=1, source_target_pairs={{8,0},{16,8},{24,16},{0,24},{9,1},{17,9},{25,17},{1,25},{10,2},{18... | collective-permute-start | bytes 466952 | tf_op jit(solution)/shard_map/ppermute | solution.py:55
  66.0 8.2 %collective-permute-start.13 = (f32[19,1,16,128]{3,2,1,0:T(8,128)S(1)}, f32[19,1,16,128]{3,2,1,0:T(8,128)S(1)}, u32[]{:S(2)}, u32[]{:S(2)}) collective-permute-start(f32[19,1,16,128]{3,2,1,0:T(8,128)S(1)} %get-tuple-element.109), channel_id=1, source_target_pairs={{0,8},{8,16},{16,24},{24,0},{1,9},{9,17},{17,25},{25,1},{2,10},{10... | collective-permute-start | bytes 466952 | tf_op jit(solution)/shard_map/ppermute | solution.py:52
  74.2 4.0 %collective-permute-start.14 = (f32[19,4,1,128]{3,2,1,0:T(1,128)S(1)}, f32[19,4,1,128]{3,2,1,0:T(1,128)S(1)}, u32[]{:S(2)}, u32[]{:S(2)}) collective-permute-start(f32[19,4,1,128]{3,2,1,0:T(1,128)S(1)} %get-tuple-element.102), channel_id=1, source_target_pairs={{4,0},{0,4},{5,1},{1,5},{6,2},{2,6},{7,3},{3,7},{12,8},{8,12},{13,... | collective-permute-start | bytes 116744 | tf_op jit(solution)/shard_map/ppermute | solution.py:55
  75.8 4.0 %collective-permute-start.15 = (f32[19,4,1,128]{3,2,1,0:T(1,128)S(1)}, f32[19,4,1,128]{3,2,1,0:T(1,128)S(1)}, u32[]{:S(2)}, u32[]{:S(2)}) collective-permute-start(f32[19,4,1,128]{3,2,1,0:T(1,128)S(1)} %get-tuple-element.101), channel_id=1, source_target_pairs={{0,4},{4,0},{1,5},{5,1},{2,6},{6,2},{3,7},{7,3},{8,12},{12,8},{9,1... | collective-permute-start | bytes 116744 | tf_op jit(solution)/shard_map/ppermute | solution.py:52
  80.8 1.7 collective-permute-start.16
  81.5 3.6 %collective-permute-start.17 = (f32[19,4,18,1]{0,1,3,2:T(4,128)S(1)}, f32[19,4,18,1]{0,1,3,2:T(4,128)S(1)}, u32[]{:S(2)}, u32[]{:S(2)}) collective-permute-start(f32[19,4,18,1]{0,1,3,2:T(4,128)S(1)} %copy.98), channel_id=1, source_target_pairs={{0,1},{1,2},{2,3},{3,0},{4,5},{5,6},{6,7},{7,4},{8,9},{9,10},{10,1... | collective-permute-start | bytes 16424 | tf_op jit(solution)/shard_map/ppermute | solution.py:52
  87.0 28.7 %collective-permute-start.18 = (f32[19,1,16,128]{3,2,1,0:T(8,128)S(1)}, f32[19,1,16,128]{3,2,1,0:T(8,128)S(1)}, u32[]{:S(2)}, u32[]{:S(2)}) collective-permute-start(f32[19,1,16,128]{3,2,1,0:T(8,128)S(1)} %get-tuple-element.108), channel_id=1, source_target_pairs={{0,8},{8,16},{16,24},{24,0},{1,9},{9,17},{17,25},{25,1},{2,10},{10... | collective-permute-start | bytes 466952 | tf_op jit(solution)/shard_map/ppermute | solution.py:52
  87.5 28.2 %collective-permute-start.19 = (f32[19,1,16,128]{3,2,1,0:T(8,128)S(1)}, f32[19,1,16,128]{3,2,1,0:T(8,128)S(1)}, u32[]{:S(2)}, u32[]{:S(2)}) collective-permute-start(f32[19,1,16,128]{3,2,1,0:T(8,128)S(1)} %get-tuple-element.107), channel_id=1, source_target_pairs={{8,0},{16,8},{24,16},{0,24},{9,1},{17,9},{25,17},{1,25},{10,2},{18... | collective-permute-start | bytes 466952 | tf_op jit(solution)/shard_map/ppermute | solution.py:55
  115.8 4.0 %collective-permute-start.20 = (f32[19,4,1,128]{3,2,1,0:T(1,128)S(1)}, f32[19,4,1,128]{3,2,1,0:T(1,128)S(1)}, u32[]{:S(2)}, u32[]{:S(2)}) collective-permute-start(f32[19,4,1,128]{3,2,1,0:T(1,128)S(1)} %get-tuple-element.100), channel_id=1, source_target_pairs={{0,4},{4,0},{1,5},{5,1},{2,6},{6,2},{3,7},{7,3},{8,12},{12,8},{9,1... | collective-permute-start | bytes 116744 | tf_op jit(solution)/shard_map/ppermute | solution.py:52
  116.4 4.0 %collective-permute-start.21 = (f32[19,4,1,128]{3,2,1,0:T(1,128)S(1)}, f32[19,4,1,128]{3,2,1,0:T(1,128)S(1)}, u32[]{:S(2)}, u32[]{:S(2)}) collective-permute-start(f32[19,4,1,128]{3,2,1,0:T(1,128)S(1)} %get-tuple-element.99), channel_id=1, source_target_pairs={{4,0},{0,4},{5,1},{1,5},{6,2},{2,6},{7,3},{3,7},{12,8},{8,12},{13,... | collective-permute-start | bytes 116744 | tf_op jit(solution)/shard_map/ppermute | solution.py:55
  121.5 3.5 %collective-permute-start.22 = (f32[19,4,18,1]{2,0,3,1:T(8,128)S(1)}, f32[19,4,18,1]{2,0,3,1:T(8,128)S(1)}, u32[]{:S(2)}, u32[]{:S(2)}) collective-permute-start(f32[19,4,18,1]{2,0,3,1:T(8,128)S(1)} %copy.100), channel_id=1, source_target_pairs={{0,1},{1,2},{2,3},{3,0},{4,5},{5,6},{6,7},{7,4},{8,9},{9,10},{10,1... | collective-permute-start | bytes 16424 | tf_op jit(solution)/shard_map/ppermute | solution.py:52
  122.2 3.5 %collective-permute-start.23 = (f32[19,4,18,1]{2,0,3,1:T(8,128)S(1)}, f32[19,4,18,1]{2,0,3,1:T(8,128)S(1)}, u32[]{:S(2)}, u32[]{:S(2)}) collective-permute-start(f32[19,4,18,1]{2,0,3,1:T(8,128)S(1)} %copy.102), channel_id=1, source_target_pairs={{1,0},{2,1},{3,2},{0,3},{5,4},{6,5},{7,6},{4,7},{9,8},{10,9},{11,1... | collective-permute-start | bytes 16424 | tf_op jit(solution)/shard_map/ppermute | solution.py:55
  127.1 81.6 %copy-start.2 = (f32[19,2,16,128]{3,2,1,0:T(8,128)}, f32[19,2,16,128]{3,2,1,0:T(8,128)S(1)}, u32[]{:S(2)}) copy-start(f32[19,2,16,128]{3,2,1,0:T(8,128)S(1)} %constant_dynamic-update-slice_fusion.152) | copy-start | bytes 933892
Sparse Core Ops, SparseCore 0:
  115.8 38.3 reduce-scatter.1
